TPU v7x, 32 devices: a whole 2x2x4 slice. The times are simulated.
32 devices in a mesh: vocab: 8 (over z, x), dp: 4 (over y, core).
Axes of the slice: x: 2, y: 2, z: 4, core: 2. Of those that a mesh axis runs over, the one named last changes fastest.
Arguments:
- teacher_hidden: bfloat16 [512, 5376], P('dp'), may hold values from -48 to 48
- student_hidden: bfloat16 [512, 2560], P('dp'), may hold values from -48 to 48
- teacher_codes: bfloat16 [16384, 5376], P(('vocab', 'dp')), may hold values from -8 to 7, as said below
- teacher_scales: float32 [16384, 42], P(('vocab', 'dp')), may hold values from 0.003 to 0.07
- student_weight: bfloat16 [16384, 2560], P(('vocab', 'dp')), may hold values from -1 to 1
- loss_scale: bfloat16 [512], P('dp'), may hold values from 2 to 20
Outputs:
- kl: float32 [512], P('dp')
- grad_hidden: bfloat16 [512, 2560], P('dp', 'vocab')
- grad_weight: bfloat16 [16384, 2560], P(('vocab', 'dp'))
Inputs may be any that keep to these rules, and one draw needn't show every extreme that they name: `teacher_codes`: whole numbers.
All inputs are finite; a program needn't handle non-finite values.
Results may differ from a plain program's by a relative error of at most 0.0085.
Values may be sent and summed in bfloat16 or wider, within the bound.
A program may use at most 128 MiB of HBM per device.

v0:
```python
import jax
import jax.numpy as jnp
from jax import lax
from jax.sharding import PartitionSpec as P

GROUP = 128


def dequantize(code_values, scales):
    row_count = code_values.shape[0]
    grouped = code_values.astype(jnp.float32).reshape(row_count, -1, GROUP) * scales[:, :, None]
    return grouped.reshape(row_count, -1).astype(jnp.bfloat16)


def contract_last(left_rows, right_rows):
    return lax.dot_general(
        left_rows, right_rows, (((1,), (1,)), ((), ())), preferred_element_type=jnp.float32
    )


def local(
    teacher_hidden, student_hidden, teacher_codes, teacher_scales, student_weight, loss_scale
):
    tok_rows = teacher_hidden.shape[0]
    teacher_all, student_all, scale_all = (
        lax.all_gather(teacher_hidden, "dp", axis=0, tiled=True),
        lax.all_gather(student_hidden, "dp", axis=0, tiled=True),
        lax.all_gather(loss_scale, "dp", axis=0, tiled=True),
    )
    teacher_table = dequantize(teacher_codes, teacher_scales)
    teacher_logits = contract_last(teacher_all, teacher_table)
    student_logits = contract_last(student_all, student_weight)
    teacher_local = jnp.max(teacher_logits, axis=1)
    student_local = jnp.max(student_logits, axis=1)
    teacher_top, student_top = lax.pmax((teacher_local, student_local), ("vocab", "dp"))
    teacher_exp = jnp.exp(teacher_logits - teacher_top[:, None])
    student_exp = jnp.exp(student_logits - student_top[:, None])
    teacher_total, cross_total, student_total = lax.psum(
        (
            jnp.sum(teacher_exp, axis=1),
            jnp.sum(teacher_exp * (teacher_logits - student_logits), axis=1),
            jnp.sum(student_exp, axis=1),
        ),
        ("vocab", "dp"),
    )
    teacher_lse = teacher_top + jnp.log(teacher_total)
    student_lse = student_top + jnp.log(student_total)
    divergence = cross_total / teacher_total - teacher_lse + student_lse
    own_start = lax.axis_index("dp") * tok_rows
    kl = lax.dynamic_slice_in_dim(divergence, own_start, tok_rows, 0)
    teacher_prob = jnp.exp(teacher_logits - teacher_lse[:, None])
    student_prob = jnp.exp(student_logits - student_lse[:, None])
    logit_grad = (scale_all.astype(jnp.float32)[:, None] * (student_prob - teacher_prob)).astype(
        jnp.bfloat16
    )
    grad_weight = lax.dot_general(
        logit_grad, student_all, (((0,), (0,)), ((), ())), preferred_element_type=jnp.float32
    ).astype(jnp.bfloat16)
    token_part = lax.psum_scatter(
        jnp.dot(logit_grad, student_weight, preferred_element_type=jnp.float32),
        "dp",
        scatter_dimension=0,
        tiled=True,
    )
    grad_hidden = lax.psum_scatter(token_part, "vocab", scatter_dimension=1, tiled=True).astype(
        jnp.bfloat16
    )
    return (kl, grad_hidden, grad_weight)


def solution(mesh):
    in_specs = (
        P("dp", None),
        P("dp", None),
        P(("vocab", "dp"), None),
        P(("vocab", "dp"), None),
        P(("vocab", "dp"), None),
        P("dp"),
    )
    out_specs = (P("dp"), P("dp", "vocab"), P(("vocab", "dp"), None))
    return jax.shard_map(local, mesh=mesh, in_specs=in_specs, out_specs=out_specs, check_vma=False)
```

profile of v0, /device:TPU:0, one launch (start us, length us, event | category | flops | bytes accessed | tf_op | source)
XLA Modules:
  0.0 305.5 jit_solution(14762963266301238189)
XLA Ops:
  7.2 0.0 copy-start
  7.2 0.0 all-gather.6.cloned.1.call-start
  7.2 0.7 all-gather.6.cloned.1.call-update
  7.9 0.0 all-gather.4.cloned.1.call-start
  8.0 0.7 all-gather.4.cloned.1.call-update
  8.7 0.0 copy-start.2
  8.7 0.0 copy-start.1
  8.7 0.0 reduce-scatter.5.cloned.1.call-start
  8.7 8.3 %copy.13 = bf16[512,5376]{0,1:T(8,128)(2,1)} copy(bf16[512,5376]{1,0:T(8,128)(2,1)} %param.8) | data formatting | bytes 11010048 | tf_op args[2]
  17.0 0.0 copy-done.2
  17.0 6.0 %all-gather = bf16[4,1,128]{2,1,0:T(2,128)(2,1)S(1)} all-gather(bf16[1,1,128]{2,1,0:T(2,128)(2,1)S(1)} %bitcast.41), channel_id=1, replica_groups=mesh['vocab'=8,'dp'=4] {'dp'}, dimensions={0}, use_global_device_ids=true | all-gather | bytes 1280 | tf_op jit(solution)/shard_map/all_gather | solution.py:28
  23.0 6.1 %fusion = bf16[512,5376]{0,1:T(8,128)(2,1)} fusion(bf16[512,5376]{0,1:T(8,128)(2,1)} %copy.13, f32[512,42]{0,1:T(8,128)S(1)} %copy-done.1), kind=kLoop, calls=%fused_computation.1 | loop fusion | flops 8257536 | bytes 11096064 | tf_op jit(solution)/shard_map/convert_element_type | solution.py:12
  29.2 8.7 %all-gather.6.cloned.1.call-done = bf16[512,2560]{1,0:T(8,128)(2,1)} async-done(((bf16[128,2560]{1,0:T(8,128)(2,1)}), bf16[512,2560]{1,0:T(8,128)(2,1)}) %all-gather.6.cloned.1.call-update) | async-done | bytes 2621456 | tf_op jit(solution)/shard_map/all_gather | solution.py:27
  37.8 0.0 copy-done
  37.8 4.3 %fusion.9 = (f32[512]{0:T(512)S(1)}, f32[512,512]{0,1:T(8,128)}) fusion(bf16[512,2560]{1,0:T(8,128)(2,1)} %all-gather.6.cloned.1.call-done, bf16[512,2560]{1,0:T(8,128)(2,1)S(1)} %copy-done), kind=kOutput, calls=%fused_computation.18 | convolution fusion | flops 1342438912 | bytes 6293504 | tf_op jit(solution)/shard_map/dot_general | solution.py:16
  42.1 39.2 %all-gather.4.cloned.1.call-done = bf16[512,5376]{1,0:T(8,128)(2,1)} async-done(((bf16[128,5376]{1,0:T(8,128)(2,1)}), bf16[512,5376]{1,0:T(8,128)(2,1)}) %all-gather.4.cloned.1.call-update) | async-done | bytes 5505040 | tf_op jit(solution)/shard_map/all_gather | solution.py:26
  81.3 8.2 %fusion.10 = (f32[512]{0:T(512)S(1)}, f32[512,512]{1,0:T(8,128)}) fusion(bf16[512,5376]{0,1:T(8,128)(2,1)} %fusion, bf16[512,5376]{1,0:T(8,128)(2,1)} %all-gather.4.cloned.1.call-done), kind=kOutput, calls=%fused_computation.19 | convolution fusion | flops 2818833920 | bytes 12060672 | tf_op jit(solution)/shard_map/dot_general | solution.py:16
  89.6 39.2 %all-reduce.1 = (f32[512]{0:T(512)S(1)}, f32[512]{0:T(512)S(1)}) all-reduce(f32[512]{0:T(512)S(1)} %get-tuple-element.23, f32[512]{0:T(512)S(1)} %get-tuple-element.25), channel_id=1, replica_groups=mesh['vocab'=8,'dp'=4] {'vocab','dp'}, use_global_device_ids=true, to_apply=%region_7.0 | all-reduce | flops 1024 | bytes 8192 | tf_op jit(solution)/shard_map/pmax | solution.py:35
  128.8 1.9 fusion.3
  130.7 41.1 %all-reduce = (f32[512]{0:T(512)S(1)}, f32[512]{0:T(512)S(1)}, f32[512]{0:T(512)S(1)}) all-reduce(f32[512]{0:T(512)S(1)} %get-tuple-element.14, f32[512]{0:T(512)S(1)} %get-tuple-element.13, f32[512]{0:T(512)S(1)} %get-tuple-element.12), channel_id=1, replica_groups=mesh['vocab'=8,'dp'=4] {'vocab','dp'}, use_global_device_ids=true, to_apply=%region_9.0 | all-reduce | flops 1536 | bytes 12288 | tf_op jit(solution)/shard_map/psum | solution.py:38
  171.8 1.8 fusion.7
  173.7 3.9 %fusion.11 = f32[512,2560]{1,0:T(8,128)} fusion(bf16[512,512]{0,1:T(8,128)(2,1)S(1)} %fusion.7, bf16[512,2560]{1,0:T(8,128)(2,1)S(1)} %copy-done), kind=kOutput, calls=%fused_computation.20 | convolution fusion | flops 1342177280 | bytes 8388608 | tf_op jit(solution)/shard_map/dot_general | solution.py:60
  177.5 0.0 reduce-scatter.5.cloned.1.call-update
  177.6 0.0 reduce-scatter.7.cloned.1.call-start
  177.6 51.2 %reduce-scatter.5.cloned.1.call-done = f32[128,2560]{1,0:T(8,128)} async-done(((f32[512,2560]{1,0:T(8,128)}), f32[128,2560]{1,0:T(8,128)}) %reduce-scatter.5.cloned.1.call-update) | async-done | bytes 1310736 | tf_op jit(solution)/shard_map/reduce_scatter | solution.py:59
  228.8 2.8 copy.15
  231.6 0.0 reduce-scatter.7.cloned.1.call-update
  231.6 0.6 dynamic_slice.3
  232.2 4.8 %convolution_convert_fusion = bf16[512,2560]{1,0:T(8,128)(2,1)} fusion(bf16[512,512]{0,1:T(8,128)(2,1)S(1)} %fusion.7, bf16[512,2560]{1,0:T(8,128)(2,1)} %all-gather.6.cloned.1.call-done), kind=kOutput, calls=%fused_computation.2 | convolution fusion | flops 1343488000 | bytes 5767168 | tf_op jit(solution)/shard_map/dot_general | solution.py:56
  236.9 60.3 %reduce-scatter.7.cloned.1.call-done = f32[320,128]{1,0:T(8,128)} async-done(((f32[2560,128]{1,0:T(8,128)}), f32[320,128]{1,0:T(8,128)}) %reduce-scatter.7.cloned.1.call-update) | async-done | bytes 163856
  297.2 1.0 copy.16
  298.2 0.8 copy.14
  (3 shorter events, 0.0 us)
Async XLA Ops:
  7.2 30.7 %copy-start = (bf16[512,2560]{1,0:T(8,128)(2,1)S(1)}, bf16[512,2560]{1,0:T(8,128)(2,1)}, u32[]{:S(2)}) copy-start(bf16[512,2560]{1,0:T(8,128)(2,1)} %param.10) | copy-start | bytes 7864324
  7.2 30.7 %all-gather.6.cloned.1.call-start = ((), (), s32[]{:S(2)}) async-start(), calls=%async_computation.3 | async-start | bytes 3276800 | tf_op jit(solution)/shard_map/all_gather | solution.py:27
  7.9 73.4 %all-gather.4.cloned.1.call-start = ((), (), s32[]{:S(2)}) async-start(), calls=%async_computation.2 | async-start | bytes 6881280 | tf_op jit(solution)/shard_map/all_gather | solution.py:26
  8.7 8.3 %copy-start.2 = (bf16[128]{0:T(256)(128)(2,1)S(1)}, bf16[128]{0:T(256)(128)(2,1)}, u32[]{:S(2)}) copy-start(bf16[128]{0:T(256)(128)(2,1)} %param.11) | copy-start | bytes 772
  8.7 14.4 %copy-start.1 = (f32[512,42]{0,1:T(8,128)S(1)}, f32[512,42]{0,1:T(8,128)}, u32[]{:S(2)}) copy-start(f32[512,42]{0,1:T(8,128)} %param.9) | copy-start | bytes 258052
  8.7 220.1 %reduce-scatter.5.cloned.1.call-start = ((), (), s32[]{:S(2)}) async-start(), calls=%async_computation.4 | async-start | bytes 6553600 | tf_op jit(solution)/shard_map/reduce_scatter | solution.py:59
  177.6 119.7 %reduce-scatter.7.cloned.1.call-start = ((), (), s32[]{:S(2)}) async-start(), calls=%async_computation.5 | async-start | bytes 1474560
Sparse Core Ops, SparseCore 0:
  9.5 28.2 all-gather.5
  39.4 41.8 all-gather.3
  177.7 51.0 reduce-scatter.4
  232.0 65.1 reduce-scatter.6
where the time goes:
time: 306 us
  waiting for transfers between devices  161 us (53%)
  blocking collectives  86.3 us (28%)
  matrix products  21.1 us (7%)
  between operations  13.8 us (5%)
  local copies, waits for them, and re-layouts  13.4 us (4%)
  other arithmetic  9.94 us (3%)
    unnamed x5, waiting for transfers between devices  61.7 us
    reduce_scatter x1, waiting for transfers between devices, local(): lax.psum_scatter(jnp.dot(logit_grad, student_weight, preferred_element_ty...  51.2 us
    psum x1, blocking collectives, local(): lax.psum((jnp.sum(teacher_exp, axis=1), jnp.sum(teacher_exp * (teacher_lo...  41.1 us
    pmax x1, blocking collectives, local(): lax.pmax((teacher_local, student_local), ('vocab', 'dp'))  39.2 us
    all_gather x1, waiting for transfers between devices, local(): lax.all_gather(teacher_hidden, 'dp', axis=0, tiled=True)  39.2 us
    unnamed x10, local copies, waits for them, and re-layouts  12.9 us
    dot_general x2, matrix products, contract_last(): lax.dot_general(left_rows, right_rows, (((1,), (1,)), ((), ())), preferre...  12.5 us
    all_gather x1, waiting for transfers between devices, local(): lax.all_gather(student_hidden, 'dp', axis=0, tiled=True)  8.66 us
  transfers between devices with their start and end apart: 4, of which 4 were waited for; matrix products, arithmetic and copies ran while one was open for 8% of the time, Pallas kernels for 0%

commit v1 on v0

v1 whole, which is shorter than its diff:
```python
import functools

import jax
import jax.numpy as jnp
from jax import lax
from jax.experimental import pallas as pl
from jax.experimental.pallas import tpu as pltpu
from jax.sharding import PartitionSpec as P

GROUP = 128
LANE = 128
MESH = pl.DeviceIdType.MESH


def step_width(cols):
    units = cols // 256
    per = max(k for k in (1, 2, 3) if units % k == 0)
    return per * 256


def dot_t(left_rows, right_rows):
    return lax.dot_general(
        left_rows, right_rows, (((1,), (1,)), ((), ())), preferred_element_type=jnp.float32
    )


def kernel(
    n_vocab, n_dp,
    th_own, sh_own, codes, scales, weight, loss,
    kl_out, gh_out, gw_out,
    th, sh, table, wgt, wgt_t, tlog, slog, lsc, stat, stat_b, fin, in_a, in_b,
    grad, gw_buf, mine, theirs, core_in,
    y1s, y1r, x1s, x1r, x2s, x2r, y2s, y2r, zs, zr, zf,
    ld_sem, gw_sem, pc_s, pc_r, ys, yr, xs, xr, d1s, d1r, d2s, d2r,
    ls_s, ls_r, a_s, a_r, b_s, b_r, cs, cr, r1s, r1r, r2s, r2r, z_ss, z_rs,
):
    v, d = lax.axis_index("vocab"), lax.axis_index("dp")
    c, y = lax.rem(d, 2), lax.div(d, 2)
    p, q = lax.rem(v, 2), lax.div(v, 2)
    n_y, n_z = n_dp // 2, n_vocab // 2
    n_off = n_y - 1
    mate = 2 * y + 1 - c
    v_pair = 2 * q + 1 - p
    tok = th_own.shape[0]
    rv = zr.shape[1]
    n_z1 = n_z // 2

    def rcopy(src, dst, send, recv, dev):
        return pltpu.make_async_remote_copy(
            src_ref=src, dst_ref=dst, send_sem=send, recv_sem=recv,
            device_id=dev, device_id_type=MESH,
        )

    chunks = []
    for own, scr, tab, acc in ((th_own, th, table, tlog), (sh_own, sh, wgt, slog)):
        width = step_width(own.shape[1])
        for base in range(0, own.shape[1], width):
            chunks.append((own, scr, tab, acc, base, width))
    n_ch = len(chunks)

    loads = []
    for k, (own, scr, tab, acc, base, width) in enumerate(chunks):
        src = codes if tab is table else weight
        cp = pltpu.make_async_copy(
            src.at[:, pl.ds(base, width)], tab.at[:, pl.ds(base, width)], ld_sem.at[k]
        )
        cp.start()
        loads.append(cp)
    own_rows = pl.ds(pl.multiple_of(d * tok, tok), tok)
    own_loads = [
        pltpu.make_async_copy(th_own, th.at[own_rows], ld_sem.at[n_ch]),
        pltpu.make_async_copy(sh_own, sh.at[own_rows], ld_sem.at[n_ch + 1]),
    ]
    for cp in own_loads:
        cp.start()

    peers_a = []
    for dv in range(2):
        for dd in range(n_dp):
            if dv or dd:
                peers_a.append((v if dv == 0 else v_pair, lax.rem(d + dd, n_dp)))
    from_a = []
    peers_b = [(2 * lax.rem(q + o, n_z) + p, d) for o in range(1, n_z)]
    barrier = pltpu.get_barrier_semaphore()
    for peer in peers_a + peers_b:
        pl.semaphore_signal(barrier, inc=1, device_id=peer, device_id_type=MESH)
    pl.semaphore_wait(barrier, len(peers_a) + len(peers_b))

    def cols(k, which):
        base, width = chunks[k][4], chunks[k][5]
        half = width // 2
        return pl.ds(pl.multiple_of(base + which * half, LANE), half)

    def rows(block):
        return pl.ds(pl.multiple_of(block * tok, tok), tok)

    def y_send(k, o):
        own, scr = chunks[k][0], chunks[k][1]
        to = 2 * lax.rem(y + o, n_y) + c
        return rcopy(
            own.at[:, cols(k, p)], scr.at[rows(d), cols(k, p)],
            ys.at[o - 1, k], yr.at[o - 1, k], (v, to),
        )

    def came(o):
        return lax.rem(y + n_y - o, n_y)

    def fwd(k, o, which, block, send, recv, dev):
        scr = chunks[k][1]
        ref = scr.at[rows(block), cols(k, which)]
        return rcopy(ref, ref, send.at[o - 1, k], recv.at[o - 1, k], dev)

    def x_fwd(k, o, which):
        return fwd(k, o, which, 2 * came(o) + c, xs, xr, (v_pair, d))

    def d1_fwd(k, o, side):
        return fwd(k, o, p, 2 * came(o) + side, d1s, d1r, (v, mate))

    def d2_fwd(k, o, side):
        return fwd(k, o, 1 - p, 2 * came(o) + side, d2s, d2r, (v, mate))

    sends = []
    mate_copies = [
        rcopy(th_own, th.at[own_rows], pc_s.at[0], pc_r.at[0], (v, mate)),
        rcopy(sh_own, sh.at[own_rows], pc_s.at[1], pc_r.at[1], (v, mate)),
    ]
    for k in range(n_ch):
        for o in range(1, n_y):
            cp = y_send(k, o)
            cp.start()
            sends.append(cp)
        if k == 0:
            for cp in mate_copies:
                cp.start()
    loss_copies = []
    for dd in range(1, n_dp):
        cp = rcopy(
            loss, lsc.at[d], ls_s.at[dd - 1], ls_r.at[dd - 1], (v, lax.rem(d + dd, n_dp))
        )
        cp.start()
        loss_copies.append(cp)
    lsc[d] = loss[...]

    def product(k, chip, first):
        own, scr, tab, acc, base, width = chunks[k]
        two = pl.ds(pl.multiple_of(chip * 2 * tok, 2 * tok), 2 * tok)
        part = dot_t(tab[:, pl.ds(base, width)], scr[two, pl.ds(base, width)])
        if first:
            acc[:, two] = part
        else:
            acc[:, two] += part

    def prepare(k):
        own, scr, tab, acc, base, width = chunks[k]
        loads[k].wait()
        if tab is table:
            @pl.loop(0, table.shape[0] // 64)
            def _(r):
                rsl = pl.ds(pl.multiple_of(r * 64, 64), 64)
                sc = scales[rsl, :]
                for g in range(width // GROUP):
                    lane = pl.ds(base + g * GROUP, GROUP)
                    col = (base + g * GROUP) // GROUP
                    wide = table[rsl, lane].astype(jnp.float32) * sc[:, col : col + 1]
                    table[rsl, lane] = wide.astype(jnp.bfloat16)
        else:
            for b in range(base, base + width, 256):
                wgt_t[pl.ds(b, 256), :] = wgt[:, pl.ds(b, 256)].T

    for cp in own_loads:
        cp.wait()
    firsts = [k == 0 or chunks[k][3] is not chunks[k - 1][3] for k in range(n_ch)]
    for k in range(n_ch + 2):
        if k < n_ch:
            prepare(k)
            for o in range(1, n_y):
                fwd(
                    k, o, p, 2 * came(o) + c, ys, yr, (v, mate)
                ).wait_recv()
                for cp in (x_fwd(k, o, p), d1_fwd(k, o, c)):
                    cp.start()
                    sends.append(cp)
        if 1 <= k <= n_ch:
            for o in range(1, n_y):
                x_fwd(k - 1, o, 1 - p).wait_recv()
                cp = d2_fwd(k - 1, o, c)
                cp.start()
                sends.append(cp)
        if k < n_ch:
            if k == 0:
                for which, (own, scr) in enumerate(((th_own, th), (sh_own, sh))):
                    land = scr.at[rows(mate)]
                    rcopy(own, land, pc_s.at[which], pc_r.at[which], (v, mate)).wait_recv()
            product(k, y, firsts[k])
        if k >= 2:
            for o in range(1, n_y):
                fwd(
                    k - 2, o, p, 2 * came(o) + 1 - c, d1s, d1r, (v, mate)
                ).wait_recv()
                fwd(
                    k - 2, o, 1 - p, 2 * came(o) + 1 - c, d2s, d2r, (v, mate)
                ).wait_recv()
            if n_y > 1:
                @pl.loop(1, n_y)
                def _(o):
                    product(k - 2, lax.rem(y + n_y - o, n_y), firsts[k - 2])

    n_tok = n_dp * tok

    @pl.loop(0, n_dp)
    def _(j):
        sl = pl.ds(pl.multiple_of(j * tok, tok), tok)
        t_max = jnp.max(tlog[:, sl], axis=0, keepdims=True)
        s_max = jnp.max(slog[:, sl], axis=0, keepdims=True)
        te = jnp.exp(tlog[:, sl] - t_max)
        t_sum = jnp.sum(te, axis=0, keepdims=True)
        x_sum = jnp.sum(te * (tlog[:, sl] - slog[:, sl]), axis=0, keepdims=True)
        tlog[:, sl] = te
        se = jnp.exp(slog[:, sl] - s_max)
        s_sum = jnp.sum(se, axis=0, keepdims=True)
        slog[:, sl] = se
        stat[:, sl] = jnp.concatenate(
            [t_max, t_sum, x_sum, s_max, s_sum, jnp.zeros((3, tok), jnp.float32)], axis=0
        )

    def merge(parts):
        t_top = functools.reduce(jnp.maximum, [x[0:1] for x in parts])
        s_top = functools.reduce(jnp.maximum, [x[3:4] for x in parts])
        t_sum = x_sum = s_sum = 0.0
        for x in parts:
            t_w = jnp.exp(x[0:1] - t_top)
            t_sum += x[1:2] * t_w
            x_sum += x[2:3] * t_w
            s_sum += x[4:5] * jnp.exp(x[3:4] - s_top)
        return t_top, t_sum, x_sum, s_top, s_sum

    for i, peer in enumerate(peers_a):
        cp = rcopy(stat, in_a.at[i], a_s.at[i], a_r.at[i], peer)
        cp.start()
        sends.append(cp)
    for i, peer in enumerate(peers_a):
        rcopy(stat, in_a.at[i], a_s.at[i], a_r.at[i], peer).wait_recv()
    stat_b[...] = jnp.concatenate(
        list(merge([stat[...]] + [in_a[i] for i in range(len(peers_a))]))
        + [jnp.zeros((3, n_tok), jnp.float32)], axis=0
    )
    for i, peer in enumerate(peers_b):
        cp = rcopy(stat_b, in_b.at[i], b_s.at[i], b_r.at[i], peer)
        cp.start()
        sends.append(cp)
    for dd in range(1, n_dp):
        other = lax.rem(d + n_dp - dd, n_dp)
        rcopy(loss, lsc.at[other], ls_s.at[dd - 1], ls_r.at[dd - 1], (v, mate)).wait_recv()
    for i, peer in enumerate(peers_b):
        rcopy(stat_b, in_b.at[i], b_s.at[i], b_r.at[i], peer).wait_recv()
    t_top, t_sum, x_sum, s_top, s_sum = merge(
        [stat_b[...]] + [in_b[i] for i in range(len(peers_b))]
    )
    t_lse = t_top + jnp.log(t_sum)
    s_lse = s_top + jnp.log(s_sum)
    fin[...] = jnp.concatenate(
        [
            x_sum / t_sum - t_lse + s_lse,
            jnp.exp(stat[0:1] - t_lse),
            jnp.exp(stat[3:4] - s_lse),
            jnp.zeros((5, n_tok), jnp.float32),
        ],
        axis=0,
    )
    kl_out[...] = fin[0:1, own_rows]

    @pl.loop(0, n_dp)
    def _(j):
        sl = pl.ds(pl.multiple_of(j * tok, tok), tok)
        f = fin[:, sl]
        grad[:, sl] = (
            lsc[j][0:1] * (slog[:, sl] * f[2:3] - tlog[:, sl] * f[1:2])
        ).astype(jnp.bfloat16)

    order = []
    for i in range(n_z1):
        order += [i, n_z1 + i]
    order += [i for i in range(n_z) if i not in order]

    def hidden_part(z):
        for pp in range(2):
            feat = wgt_t[pl.ds((2 * z + pp) * rv, rv), :]
            for yy in range(n_y):
                part = jnp.dot(
                    feat, grad[:, pl.ds(yy * 2 * tok, 2 * tok)],
                    preferred_element_type=jnp.float32,
                )
                left, right = part[:, :tok], part[:, tok:]
                mine[z, pp, yy] = jnp.where(c == 0, left, right)
                theirs[z, pp, yy] = jnp.where(c == 0, right, left).astype(jnp.bfloat16)

    def core_copy(z):
        return rcopy(theirs.at[z], core_in.at[z], cs.at[z], cr.at[z], (v, mate))

    def launch(cp):
        cp.start()
        sends.append(cp)

    def y1_copy(z, o):
        to = 2 * lax.rem(y + o, n_y) + c
        return rcopy(
            y1s.at[z, o - 1], y1r.at[z, o - 1], r1s.at[z, o - 1], r1r.at[z, o - 1], (v, to)
        )

    def x1_copy(z):
        return rcopy(x1s.at[z], x1r.at[z], r2s.at[z, 0], r2r.at[z, 0], (v_pair, d))

    def x2_copy(z):
        return rcopy(
            x2s.at[z - n_z1], x2r.at[z - n_z1], r1s.at[z, 0], r1r.at[z, 0], (v_pair, d)
        )

    def y2_copy(z, o):
        to = 2 * lax.rem(y + o, n_y) + c
        return rcopy(
            y2s.at[z - n_z1, o - 1], y2r.at[z - n_z1, o - 1],
            r2s.at[z, o - 1], r2r.at[z, o - 1], (v, to),
        )

    def after_core(z):
        core_copy(z).wait_recv()
        if z < n_z1:
            for o in range(1, n_y):
                to = lax.rem(y + o, n_y)
                for pp in range(2):
                    y1s[z, o - 1, pp] = (
                        mine[z, pp, to] + core_in[z, pp, to].astype(jnp.float32)
                    ).astype(jnp.bfloat16)
                launch(y1_copy(z, o))
        else:
            for yy in range(n_y):
                x2s[z - n_z1, yy] = (
                    mine[z, 1 - p, yy] + core_in[z, 1 - p, yy].astype(jnp.float32)
                ).astype(jnp.bfloat16)
            launch(x2_copy(z))

    def after_first(z):
        if z < n_z1:
            for o in range(1, n_y):
                y1_copy(z, o).wait_recv()

            def total(which):
                out = mine[z, which, y] + core_in[z, which, y].astype(jnp.float32)
                for o in range(1, n_y):
                    out += y1r[z, o - 1, which].astype(jnp.float32)
                return out

            x1s[z] = total(1 - p).astype(jnp.bfloat16)
            launch(x1_copy(z))
            zf[z] = total(p)
        else:
            x2_copy(z).wait_recv()

            def total(yy):
                return (
                    mine[z, p, yy] + core_in[z, p, yy].astype(jnp.float32)
                    + x2r[z - n_z1, yy].astype(jnp.float32)
                )

            for o in range(1, n_y):
                y2s[z - n_z1, o - 1] = total(lax.rem(y + o, n_y)).astype(jnp.bfloat16)
                launch(y2_copy(z, o))
            zf[z] = total(y)

    def z_copy(z):
        return rcopy(zs.at[z], zr.at[q], z_ss.at[z], z_rs.at[q], (2 * z + p, d))

    def after_second(z):
        if z < n_z1:
            x1_copy(z).wait_recv()
            full = zf[z] + x1r[z].astype(jnp.float32)
        else:
            full = zf[z]
            for o in range(1, n_y):
                y2_copy(z, o).wait_recv()
                full += y2r[z - n_z1, o - 1].astype(jnp.float32)
        zf[z] = full
        zs[z] = full.astype(jnp.bfloat16)

        @pl.when(q != z)
        def _():
            z_copy(z).start()

    n_gw = sh.shape[1] // 512
    gw_copies = []

    def weight_part(b):
        sl = pl.ds(b * 512, 512)
        gw_buf[:, sl] = jnp.dot(
            grad[...], sh[:, sl], preferred_element_type=jnp.float32
        ).astype(jnp.bfloat16)
        cp = pltpu.make_async_copy(gw_buf.at[:, sl], gw_out.at[:, sl], gw_sem.at[b])
        cp.start()
        gw_copies.append(cp)

    for z in order:
        hidden_part(z)
        launch(core_copy(z))
    for z in order:
        after_core(z)
    for b in range(n_gw):
        weight_part(b)
    for z in order:
        after_first(z)
    for z in order:
        after_second(z)
    zf_q = zf[q]
    mine_sum = [zf_q]
    total = zf_q
    for o in range(1, n_z):
        src = lax.rem(q + o, n_z)
        rcopy(zs.at[src], zr.at[src], z_ss.at[src], z_rs.at[src], (v_pair, d)).wait_recv()
        total += zr[src].astype(jnp.float32)
    gh_out[...] = total.T.astype(jnp.bfloat16)

    for cp in sends + loss_copies + mate_copies:
        cp.wait_send()
    for o in range(1, n_z):
        dst = lax.rem(q + o, n_z)
        rcopy(zs.at[dst], zr.at[q], z_ss.at[dst], z_rs.at[q], (2 * dst + p, d)).wait_send()
    for cp in gw_copies:
        cp.wait()


def solution(mesh):
    n_vocab, n_dp = mesh.shape["vocab"], mesh.shape["dp"]

    def local(th_own, sh_own, codes, scales, weight, loss_scale):
        tok, dt = th_own.shape
        ds_ = sh_own.shape[1]
        rows = codes.shape[0]
        n_tok = tok * n_dp
        n_y, n_z = n_dp // 2, n_vocab // 2
        n_off, n_z1 = n_y - 1, n_z // 2
        n_z2 = n_z - n_z1
        rv = ds_ // n_vocab
        n_ch = dt // step_width(dt) + ds_ // step_width(ds_)
        n_a, n_b = 2 * n_dp - 1, n_z - 1
        bf, f32 = jnp.bfloat16, jnp.float32
        V, D = pltpu.VMEM, pltpu.SemaphoreType.DMA
        loss = jnp.broadcast_to(loss_scale.astype(f32)[None, :], (8, tok))
        any_spec = pl.BlockSpec(memory_space=pl.ANY)
        vm_spec = pl.BlockSpec(memory_space=pltpu.VMEM)
        kl, gh, gw = pl.pallas_call(
            functools.partial(kernel, n_vocab, n_dp),
            out_shape=(
                jax.ShapeDtypeStruct((1, tok), f32),
                jax.ShapeDtypeStruct((tok, rv), bf),
                jax.ShapeDtypeStruct((rows, ds_), bf),
            ),
            in_specs=[any_spec, any_spec, any_spec, vm_spec, any_spec, vm_spec],
            out_specs=(vm_spec, vm_spec, any_spec),
            scratch_shapes=[
                V((n_tok, dt), bf), V((n_tok, ds_), bf), V((rows, dt), bf), V((rows, ds_), bf),
                V((ds_, rows), bf), V((rows, n_tok), f32), V((rows, n_tok), f32),
                V((n_dp, 8, tok), f32), V((8, n_tok), f32), V((8, n_tok), f32),
                V((8, n_tok), f32), V((n_a, 8, n_tok), f32), V((n_b, 8, n_tok), f32),
                V((rows, n_tok), bf), V((rows, ds_), bf),
                V((n_z, 2, n_y, rv, tok), f32), V((n_z, 2, n_y, rv, tok), bf),
                V((n_z, 2, n_y, rv, tok), bf),
                V((n_z1, n_off, 2, rv, tok), bf), V((n_z1, n_off, 2, rv, tok), bf),
                V((n_z1, rv, tok), bf), V((n_z1, rv, tok), bf),
                V((n_z2, n_y, rv, tok), bf), V((n_z2, n_y, rv, tok), bf),
                V((n_z2, n_off, rv, tok), bf), V((n_z2, n_off, rv, tok), bf),
                V((n_z, rv, tok), bf), V((n_z, rv, tok), bf), V((n_z, rv, tok), f32),
                D((n_ch + 2,)), D((ds_ // 512,)), D((2,)), D((2,)),
                *[D((n_off, n_ch))] * 8,
                D((n_dp - 1,)), D((n_dp - 1,)), D((n_a,)), D((n_a,)), D((n_b,)), D((n_b,)),
                D((n_z,)), D((n_z,)), *[D((n_z, n_off))] * 4, D((n_z,)), D((n_z,)),
            ],
            compiler_params=pltpu.CompilerParams(
                collective_id=0, has_side_effects=True, vmem_limit_bytes=60 * 1024 * 1024
            ),
            name="distill",
        )(th_own, sh_own, codes, scales, weight, loss)
        return kl.reshape(tok), gh, gw

    in_specs = (
        P("dp", None),
        P("dp", None),
        P(("vocab", "dp"), None),
        P(("vocab", "dp"), None),
        P(("vocab", "dp"), None),
        P("dp"),
    )
    out_specs = (P("dp"), P("dp", "vocab"), P(("vocab", "dp"), None))
    return jax.shard_map(local, mesh=mesh, in_specs=in_specs, out_specs=out_specs, check_vma=False)
```

time: 306 us -> 89 us (0.29)
  waiting for transfers between devices: 161 us -> 0 us
  blocking collectives: 86.3 us -> 0 us
  Pallas kernels: 0 us -> 78.9 us
  matrix products: 21.1 us -> 0 us
  between operations: 13.8 us -> 0.64 us
  other arithmetic: 9.94 us -> 0 us
  local copies, waits for them, and re-layouts: 13.4 us -> 9.19 us
    pallas_call x0 -> x1, Pallas kernels: none -> 78.9 us  [local(): pl.pallas_call(functools.partial(kernel, n_vocab, n_dp), out_shape=(jax.S...]
    unnamed x5 -> x0, waiting for transfers between devices: 61.7 us -> none
    reduce_scatter x1 -> x0, waiting for transfers between devices: 51.2 us -> none  [local(): lax.psum_scatter(jnp.dot(logit_grad, student_weight, preferred_element_ty...]
    all_gather x2 -> x0, waiting for transfers between devices: 47.9 us -> none  [the longest x1 39.2 us: local(): lax.all_gather(teacher_hidden, 'dp', axis=0, tiled=True)]
    psum x1 -> x0, blocking collectives: 41.1 us -> none  [local(): lax.psum((jnp.sum(teacher_exp, axis=1), jnp.sum(teacher_exp * (teacher_lo...]
    pmax x1 -> x0, blocking collectives: 39.2 us -> none  [local(): lax.pmax((teacher_local, student_local), ('vocab', 'dp'))]
    dot_general x4 -> x0, matrix products: 21.1 us -> none  [the longest x2 12.5 us: contract_last(): lax.dot_general(left_rows, right_rows, (((1,), (1,)), ((), ())), preferre...]
    convert_element_type x3 -> x0, other arithmetic: 8 us -> none  [the longest x1 6.14 us: dequantize(): return grouped.reshape(row_count, -1).astype(jnp.bfloat16)]
  transfers between devices with their start and end apart: 4 -> 0, of which waited for: 4 -> 0; matrix products, arithmetic and copies ran while one was open for 8% -> 0% of each run, Pallas kernels for 0% -> 0%
where the time goes in v1:
time: 89 us; the launch traced here: 88.7 us
  Pallas kernels  78.9 us (89%)
  local copies, waits for them, and re-layouts  9.19 us (10%)
    pallas_call x1, Pallas kernels, local(): pl.pallas_call(functools.partial(kernel, n_vocab, n_dp), out_shape=(jax.S...  78.9 us
    unnamed x4, local copies, waits for them, and re-layouts  7.94 us

profile of v1, /device:TPU:0, one launch (start us, length us, event | category | flops | bytes accessed | tf_op | source)
XLA Modules:
  0.0 88.7 jit_solution(12720299057676120678)
XLA Ops:
  0.6 1.2 %broadcast_in_dim.2.loss = f32[8,128]{1,0:T(8,128)} broadcast(bf16[128]{0:T(256)(128)(2,1)} %param.11), dimensions={1} | broadcast | bytes 4352 | tf_op jit(solution)/shard_map/broadcast_in_dim | solution.py:446
  1.9 1.7 %copy.9.scales = f32[512,42]{1,0:T(8,128)} copy(f32[512,42]{0,1:T(8,128)} %param.9) | data formatting | bytes 172032 | tf_op args[3]
  3.6 78.9 %distill.1 = (f32[1,128]{1,0:T(1,128)}, bf16[128,320]{1,0:T(8,128)(2,1)}, bf16[512,2560]{1,0:T(8,128)(2,1)}) custom-call(bf16[128,5376]{1,0:T(8,128)(2,1)} %th_own.1, bf16[128,2560]{1,0:T(8,128)(2,1)} %sh_own.1, bf16[512,5376]{1,0:T(8,128)(2,1)} %codes.1, f32[512,42]{1,0:T(8,128)} %copy.9.scales, bf16[512,2560]{1,0:T(8,128)(2,1)} %weight.1, ...), custom_call_target="tpu_custom_call" | custom-call | tf_op jit(solution)/shard_map/distill/pallas_call | solution.py:449
  82.5 1.6 %copy.10 = bf16[128,320]{0,1:T(8,128)(2,1)} copy(bf16[128,320]{1,0:T(8,128)(2,1)} %get-tuple-element.10) | data formatting | bytes 163840
  84.2 1.2 %copy.13 = f32[128]{0:T(128)} copy(f32[128]{0:T(128)} %bitcast.1) | data formatting | bytes 1024
  85.3 3.4 %copy.14 = bf16[512,2560]{1,0:T(8,128)(2,1)} copy(bf16[512,2560]{1,0:T(8,128)(2,1)} %get-tuple-element.17) | data formatting | bytes 5242880

commit v2 on v1

--- a/solution.py
+++ b/solution.py
@@ -26,12 +26,12 @@
 
 def kernel(
     n_vocab, n_dp,
-    th_own, sh_own, codes, scales, weight, loss,
+    th_own, sh_own, codes, scales, weight, loss_in,
     kl_out, gh_out, gw_out,
     th, sh, table, wgt, wgt_t, tlog, slog, lsc, stat, stat_b, fin, in_a, in_b,
     grad, gw_buf, mine, theirs, core_in,
     y1s, y1r, x1s, x1r, x2s, x2r, y2s, y2r, zs, zr, zf,
-    ld_sem, gw_sem, pc_s, pc_r, ys, yr, xs, xr, d1s, d1r, d2s, d2r,
+    sc_rows, loss_row, ld_sem, gw_sem, pc_s, pc_r, hop_s, hop_r,
     ls_s, ls_r, a_s, a_r, b_s, b_r, cs, cr, r1s, r1r, r2s, r2r, z_ss, z_rs,
 ):
     v, d = lax.axis_index("vocab"), lax.axis_index("dp")
@@ -41,6 +41,8 @@
     n_off = n_y - 1
     mate = 2 * y + 1 - c
     v_pair = 2 * q + 1 - p
+    r = lax.rem(q, 2)
+    v_quad = 2 * (q + 1 - 2 * r) + p
     tok = th_own.shape[0]
     rv = zr.shape[1]
     n_z1 = n_z // 2
@@ -86,38 +88,80 @@
         pl.semaphore_signal(barrier, inc=1, device_id=peer, device_id_type=MESH)
     pl.semaphore_wait(barrier, len(peers_a) + len(peers_b))
 
-    def cols(k, which):
-        base, width = chunks[k][4], chunks[k][5]
-        half = width // 2
-        return pl.ds(pl.multiple_of(base + which * half, LANE), half)
+    quarter = tok // 4
 
     def rows(block):
         return pl.ds(pl.multiple_of(block * tok, tok), tok)
 
-    def y_send(k, o):
-        own, scr = chunks[k][0], chunks[k][1]
+    def region(k, block, piece, half=None):
+        scr, base, width = chunks[k][1], chunks[k][4], chunks[k][5]
+        first, size = block * tok + piece * quarter, quarter
+        if half is not None:
+            size = quarter // 2
+            first += half * size
+        return scr.at[pl.ds(pl.multiple_of(first, size), size), pl.ds(base, width)]
+
+    A, B, C, E = 2 * r + p, 2 * r + 1 - p, 2 * (1 - r) + p, 2 * (1 - r) + 1 - p
+    X, Z = (v_pair, d), (v_quad, d)
+    Y_A, Y_E, X_A, Z_A, X_C, Z_B, D_A, D_B, D_C, D_E = range(10)
+
+    def far_by_y(k):
+        return k % 3 == 2
+
+    def came(o):
+        return lax.rem(y + n_y - o, n_y)
+
+    def y_send(k, o, kind):
+        own, base, width = chunks[k][0], chunks[k][4], chunks[k][5]
+        piece = A if kind == Y_A else E
+        src = own.at[pl.ds(pl.multiple_of(piece * quarter, quarter), quarter), pl.ds(base, width)]
         to = 2 * lax.rem(y + o, n_y) + c
         return rcopy(
-            own.at[:, cols(k, p)], scr.at[rows(d), cols(k, p)],
-            ys.at[o - 1, k], yr.at[o - 1, k], (v, to),
-        )
-
-    def came(o):
-        return lax.rem(y + n_y - o, n_y)
-
-    def fwd(k, o, which, block, send, recv, dev):
-        scr = chunks[k][1]
-        ref = scr.at[rows(block), cols(k, which)]
-        return rcopy(ref, ref, send.at[o - 1, k], recv.at[o - 1, k], dev)
-
-    def x_fwd(k, o, which):
-        return fwd(k, o, which, 2 * came(o) + c, xs, xr, (v_pair, d))
-
-    def d1_fwd(k, o, side):
-        return fwd(k, o, p, 2 * came(o) + side, d1s, d1r, (v, mate))
-
-    def d2_fwd(k, o, side):
-        return fwd(k, o, 1 - p, 2 * came(o) + side, d2s, d2r, (v, mate))
+            src, region(k, d, piece), hop_s.at[kind, o - 1, k], hop_r.at[kind, o - 1, k], (v, to)
+        )
+
+    def hop(kind, k, o, side, piece, dev, half=None):
+        ref = region(k, 2 * came(o) + side, piece, half)
+        return rcopy(ref, ref, hop_s.at[kind, o - 1, k], hop_r.at[kind, o - 1, k], dev)
+
+    def to_mate(kind, k, o, piece):
+        launch(hop(kind, k, o, c, piece, (v, mate)))
+
+    def launch(cp):
+        cp.start()
+        sends.append(cp)
+
+    def stage_y(k):
+        for o in range(1, n_y):
+            hop(Y_A, k, o, c, A, X).wait_recv()
+            launch(hop(X_A, k, o, c, A, X))
+            launch(hop(Z_A, k, o, c, A, Z))
+            to_mate(D_A, k, o, A)
+
+    def stage_xz(k):
+        for o in range(1, n_y):
+            hop(X_A, k, o, c, B, X).wait_recv()
+            if not far_by_y(k):
+                launch(hop(Z_B, k, o, c, B, Z, 1))
+            to_mate(D_B, k, o, B)
+            hop(Z_A, k, o, c, C, Z).wait_recv()
+            if not far_by_y(k):
+                launch(hop(X_C, k, o, c, C, X, 0))
+            to_mate(D_C, k, o, C)
+
+    def stage_far(k):
+        for o in range(1, n_y):
+            if far_by_y(k):
+                hop(Y_E, k, o, c, E, X).wait_recv()
+            else:
+                hop(X_C, k, o, c, E, X, 0).wait_recv()
+                hop(Z_B, k, o, c, E, Z, 1).wait_recv()
+            to_mate(D_E, k, o, E)
+
+    def stage_mate(k):
+        for o in range(1, n_y):
+            for kind, piece in ((D_A, A), (D_B, B), (D_C, C), (D_E, E)):
+                hop(kind, k, o, 1 - c, piece, X).wait_recv()
 
     sends = []
     mate_copies = [
@@ -126,20 +170,23 @@
     ]
     for k in range(n_ch):
         for o in range(1, n_y):
-            cp = y_send(k, o)
-            cp.start()
-            sends.append(cp)
+            launch(y_send(k, o, Y_A))
+            if far_by_y(k):
+                launch(y_send(k, o, Y_E))
         if k == 0:
             for cp in mate_copies:
                 cp.start()
     loss_copies = []
-    for dd in range(1, n_dp):
-        cp = rcopy(
-            loss, lsc.at[d], ls_s.at[dd - 1], ls_r.at[dd - 1], (v, lax.rem(d + dd, n_dp))
-        )
-        cp.start()
-        loss_copies.append(cp)
-    lsc[d] = loss[...]
+    loss_row[...] = jnp.broadcast_to(
+        loss_in[...].astype(jnp.float32).reshape(1, tok), loss_row.shape
+    )
+    lsc[d] = loss_row[...]
+    groups = scales.shape[0]
+    pad = jnp.zeros((sc_rows.shape[1] - groups, LANE), jnp.float32)
+    for b in range(0, scales.shape[1], LANE):
+        sc_rows[pl.ds(b, LANE), :] = jnp.concatenate(
+            [scales[:, pl.ds(b, LANE)], pad], axis=0
+        ).T
 
     def product(k, chip, first):
         own, scr, tab, acc, base, width = chunks[k]
@@ -155,55 +202,47 @@
         loads[k].wait()
         if tab is table:
             @pl.loop(0, table.shape[0] // 64)
-            def _(r):
-                rsl = pl.ds(pl.multiple_of(r * 64, 64), 64)
-                sc = scales[rsl, :]
+            def _(i):
+                rsl = pl.ds(pl.multiple_of(i * 64, 64), 64)
+                sc = sc_rows[rsl, :]
                 for g in range(width // GROUP):
                     lane = pl.ds(base + g * GROUP, GROUP)
                     col = (base + g * GROUP) // GROUP
                     wide = table[rsl, lane].astype(jnp.float32) * sc[:, col : col + 1]
                     table[rsl, lane] = wide.astype(jnp.bfloat16)
-        else:
-            for b in range(base, base + width, 256):
-                wgt_t[pl.ds(b, 256), :] = wgt[:, pl.ds(b, 256)].T
 
     for cp in own_loads:
         cp.wait()
     firsts = [k == 0 or chunks[k][3] is not chunks[k - 1][3] for k in range(n_ch)]
-    for k in range(n_ch + 2):
+    lag = 3
+    for k in range(n_ch + lag):
         if k < n_ch:
             prepare(k)
-            for o in range(1, n_y):
-                fwd(
-                    k, o, p, 2 * came(o) + c, ys, yr, (v, mate)
-                ).wait_recv()
-                for cp in (x_fwd(k, o, p), d1_fwd(k, o, c)):
-                    cp.start()
-                    sends.append(cp)
+            stage_y(k)
         if 1 <= k <= n_ch:
-            for o in range(1, n_y):
-                x_fwd(k - 1, o, 1 - p).wait_recv()
-                cp = d2_fwd(k - 1, o, c)
-                cp.start()
-                sends.append(cp)
+            stage_xz(k - 1)
+        if 2 <= k <= n_ch + 1:
+            stage_far(k - 2)
         if k < n_ch:
             if k == 0:
                 for which, (own, scr) in enumerate(((th_own, th), (sh_own, sh))):
                     land = scr.at[rows(mate)]
                     rcopy(own, land, pc_s.at[which], pc_r.at[which], (v, mate)).wait_recv()
             product(k, y, firsts[k])
-        if k >= 2:
-            for o in range(1, n_y):
-                fwd(
-                    k - 2, o, p, 2 * came(o) + 1 - c, d1s, d1r, (v, mate)
-                ).wait_recv()
-                fwd(
-                    k - 2, o, 1 - p, 2 * came(o) + 1 - c, d2s, d2r, (v, mate)
-                ).wait_recv()
+        if k >= lag:
+            stage_mate(k - lag)
             if n_y > 1:
                 @pl.loop(1, n_y)
                 def _(o):
-                    product(k - 2, lax.rem(y + n_y - o, n_y), firsts[k - 2])
+                    product(k - lag, lax.rem(y + n_y - o, n_y), firsts[k - lag])
+        if k == n_ch - 1:
+            for dd in range(1, n_dp):
+                cp = rcopy(
+                    loss_row, lsc.at[d], ls_s.at[dd - 1], ls_r.at[dd - 1],
+                    (v, lax.rem(d + dd, n_dp)),
+                )
+                cp.start()
+                loss_copies.append(cp)
 
     n_tok = n_dp * tok
 
@@ -238,6 +277,8 @@
         cp = rcopy(stat, in_a.at[i], a_s.at[i], a_r.at[i], peer)
         cp.start()
         sends.append(cp)
+    for b in range(0, wgt.shape[1], 256):
+        wgt_t[pl.ds(b, 256), :] = wgt[:, pl.ds(b, 256)].T
     for i, peer in enumerate(peers_a):
         rcopy(stat, in_a.at[i], a_s.at[i], a_r.at[i], peer).wait_recv()
     stat_b[...] = jnp.concatenate(
@@ -250,7 +291,7 @@
         sends.append(cp)
     for dd in range(1, n_dp):
         other = lax.rem(d + n_dp - dd, n_dp)
-        rcopy(loss, lsc.at[other], ls_s.at[dd - 1], ls_r.at[dd - 1], (v, mate)).wait_recv()
+        rcopy(loss_row, lsc.at[other], ls_s.at[dd - 1], ls_r.at[dd - 1], (v, mate)).wait_recv()
     for i, peer in enumerate(peers_b):
         rcopy(stat_b, in_b.at[i], b_s.at[i], b_r.at[i], peer).wait_recv()
     t_top, t_sum, x_sum, s_top, s_sum = merge(
@@ -296,10 +337,6 @@
 
     def core_copy(z):
         return rcopy(theirs.at[z], core_in.at[z], cs.at[z], cr.at[z], (v, mate))
-
-    def launch(cp):
-        cp.start()
-        sends.append(cp)
 
     def y1_copy(z, o):
         to = 2 * lax.rem(y + o, n_y) + c
@@ -416,7 +453,7 @@
         src = lax.rem(q + o, n_z)
         rcopy(zs.at[src], zr.at[src], z_ss.at[src], z_rs.at[src], (v_pair, d)).wait_recv()
         total += zr[src].astype(jnp.float32)
-    gh_out[...] = total.T.astype(jnp.bfloat16)
+    gh_out[...] = total.astype(jnp.bfloat16)
 
     for cp in sends + loss_copies + mate_copies:
         cp.wait_send()
@@ -425,6 +462,38 @@
         rcopy(zs.at[dst], zr.at[q], z_ss.at[dst], z_rs.at[q], (2 * dst + p, d)).wait_send()
     for cp in gw_copies:
         cp.wait()
+
+
+def hand_over(kl, gh, gw):
+    parts = 4
+    step = gw.shape[0] // parts
+
+    def move(kl_in, gh_in, gw_in, kl_to, gh_to, gw_to, kl_v, gh_v, gw_v, sem_in, sem_out):
+        plan = [(kl_in, kl_v, kl_to), (gh_in, gh_v, gh_to)]
+        for i in range(parts):
+            sl = pl.ds(i * step, step)
+            plan.append((gw_in.at[sl], gw_v.at[sl], gw_to.at[sl]))
+        reads = [pltpu.make_async_copy(a, b, sem_in.at[i]) for i, (a, b, _) in enumerate(plan)]
+        writes = [pltpu.make_async_copy(b, e, sem_out.at[i]) for i, (_, b, e) in enumerate(plan)]
+        for cp in reads:
+            cp.start()
+        for cp, out in zip(reads, writes):
+            cp.wait()
+            out.start()
+        for out in writes:
+            out.wait()
+
+    spec = pl.BlockSpec(memory_space=pl.ANY)
+    arrays = (kl, gh, gw)
+    return pl.pallas_call(
+        move,
+        out_shape=tuple(jax.ShapeDtypeStruct(a.shape, a.dtype) for a in arrays),
+        in_specs=[spec] * 3,
+        out_specs=(spec,) * 3,
+        scratch_shapes=[pltpu.VMEM(a.shape, a.dtype) for a in arrays]
+        + [pltpu.SemaphoreType.DMA((parts + 2,))] * 2,
+        name="hand_over",
+    )(*arrays)
 
 
 def solution(mesh):
@@ -443,14 +512,13 @@
         n_a, n_b = 2 * n_dp - 1, n_z - 1
         bf, f32 = jnp.bfloat16, jnp.float32
         V, D = pltpu.VMEM, pltpu.SemaphoreType.DMA
-        loss = jnp.broadcast_to(loss_scale.astype(f32)[None, :], (8, tok))
         any_spec = pl.BlockSpec(memory_space=pl.ANY)
         vm_spec = pl.BlockSpec(memory_space=pltpu.VMEM)
         kl, gh, gw = pl.pallas_call(
             functools.partial(kernel, n_vocab, n_dp),
             out_shape=(
                 jax.ShapeDtypeStruct((1, tok), f32),
-                jax.ShapeDtypeStruct((tok, rv), bf),
+                jax.ShapeDtypeStruct((rv, tok), bf),
                 jax.ShapeDtypeStruct((rows, ds_), bf),
             ),
             in_specs=[any_spec, any_spec, any_spec, vm_spec, any_spec, vm_spec],
@@ -468,8 +536,9 @@
                 V((n_z2, n_y, rv, tok), bf), V((n_z2, n_y, rv, tok), bf),
                 V((n_z2, n_off, rv, tok), bf), V((n_z2, n_off, rv, tok), bf),
                 V((n_z, rv, tok), bf), V((n_z, rv, tok), bf), V((n_z, rv, tok), f32),
+                V((rows, -(-scales.shape[1] // 8) * 8), f32), V((8, tok), f32),
                 D((n_ch + 2,)), D((ds_ // 512,)), D((2,)), D((2,)),
-                *[D((n_off, n_ch))] * 8,
+                D((10, n_off, n_ch)), D((10, n_off, n_ch)),
                 D((n_dp - 1,)), D((n_dp - 1,)), D((n_a,)), D((n_a,)), D((n_b,)), D((n_b,)),
                 D((n_z,)), D((n_z,)), *[D((n_z, n_off))] * 4, D((n_z,)), D((n_z,)),
             ],
@@ -477,8 +546,9 @@
                 collective_id=0, has_side_effects=True, vmem_limit_bytes=60 * 1024 * 1024
             ),
             name="distill",
-        )(th_own, sh_own, codes, scales, weight, loss)
-        return kl.reshape(tok), gh, gw
+        )(th_own, sh_own, codes, scales.T, weight, loss_scale)
+        kl, gh, gw = hand_over(kl, gh, gw)
+        return kl.reshape(tok), gh.T, gw
 
     in_specs = (
         P("dp", None),

time: 89 us -> 79.6 us (0.89)
  local copies, waits for them, and re-layouts: 9.19 us -> 0 us
    unnamed x4 -> x0, local copies, waits for them, and re-layouts: 7.94 us -> none
    pallas_call x1, Pallas kernels: 78.9 us -> 76 us  [local(): pl.pallas_call(functools.partial(kernel, n_vocab, n_dp), out_shape=(jax.S...]
    pallas_call x0 -> x1, Pallas kernels: none -> 2.73 us  [hand_over(): pl.pallas_call(move, out_shape=tuple((jax.ShapeDtypeStruct(a.shape, a.dty...]
    broadcast_in_dim x1 -> x0, local copies, waits for them, and re-layouts: 1.25 us -> none  [local(): loss = jnp.broadcast_to(loss_scale.astype(f32)[None, :], (8, tok))]
where the time goes in v2:
time: 79.6 us; the launch traced here: 79.4 us
  Pallas kernels  78.7 us (99%)
    pallas_call x1, Pallas kernels, local(): pl.pallas_call(functools.partial(kernel, n_vocab, n_dp), out_shape=(jax.S...  76 us
    pallas_call x1, Pallas kernels, hand_over(): pl.pallas_call(move, out_shape=tuple((jax.ShapeDtypeStruct(a.shape, a.dty...  2.73 us

profile of v2, /device:TPU:0, one launch (start us, length us, event | category | flops | bytes accessed | tf_op | source)
XLA Modules:
  0.0 79.4 jit_solution(2349267869406422039)
XLA Ops:
  0.6 76.0 %distill.1 = (f32[1,128]{1,0:T(1,128)}, bf16[320,128]{1,0:T(8,128)(2,1)}, bf16[512,2560]{1,0:T(8,128)(2,1)}) custom-call(bf16[128,5376]{1,0:T(8,128)(2,1)} %th_own.1, bf16[128,2560]{1,0:T(8,128)(2,1)} %sh_own.1, bf16[512,5376]{1,0:T(8,128)(2,1)} %codes.1, f32[42,512]{1,0:T(8,128)} %bitcast.3, bf16[512,2560]{1,0:T(8,128)(2,1)} %weight.1, bf16[128]{0:T(256)(128)(2,1)} %loss_in.1), custom_call_target="tpu_custom_call" | custom-call | tf_op jit(solution)/shard_map/distill/pallas_call | solution.py:517
  76.6 2.7 %hand_over.1 = (f32[1,128]{1,0:T(1,128)}, bf16[320,128]{1,0:T(8,128)(2,1)}, bf16[512,2560]{1,0:T(8,128)(2,1)}) custom-call(f32[1,128]{1,0:T(1,128)} %get-tuple-element.9.kl_in, bf16[320,128]{1,0:T(8,128)(2,1)} %get-tuple-element.10.gh_in, bf16[512,2560]{1,0:T(8,128)(2,1)} %get-tuple-element.11.gw_in), custom_call_target="tpu_custom_call" | custom-call | tf_op jit(solution)/shard_map/hand_over/pallas_call | solution.py:488

commit v3 on v2

--- a/solution.py
+++ b/solution.py
@@ -14,7 +14,7 @@
 
 def step_width(cols):
     units = cols // 256
-    per = max(k for k in (1, 2, 3) if units % k == 0)
+    per = max(k for k in (1, 2, 3, 5, 7) if units % k == 0)
     return per * 256
 
 
@@ -106,7 +106,7 @@
     Y_A, Y_E, X_A, Z_A, X_C, Z_B, D_A, D_B, D_C, D_E = range(10)
 
     def far_by_y(k):
-        return k % 3 == 2
+        return k > 0 and k % 2 == 0
 
     def came(o):
         return lax.rem(y + n_y - o, n_y)

time: 79.6 us -> 67.3 us (0.85)
  Pallas kernels: 78.7 us -> 66.5 us
    pallas_call x1, Pallas kernels: 76 us -> 63.8 us  [local(): pl.pallas_call(functools.partial(kernel, n_vocab, n_dp), out_shape=(jax.S...]
where the time goes in v3:
time: 67.3 us; the launch traced here: 67.2 us
  Pallas kernels  66.5 us (99%)
    pallas_call x1, Pallas kernels, local(): pl.pallas_call(functools.partial(kernel, n_vocab, n_dp), out_shape=(jax.S...  63.8 us
    pallas_call x1, Pallas kernels, hand_over(): pl.pallas_call(move, out_shape=tuple((jax.ShapeDtypeStruct(a.shape, a.dty...  2.73 us

profile of v3, /device:TPU:0, one launch (start us, length us, event | category | flops | bytes accessed | tf_op | source)
XLA Modules:
  0.0 67.2 jit_solution(2281199547502548004)
XLA Ops:
  0.6 63.8 %distill.1 = (f32[1,128]{1,0:T(1,128)}, bf16[320,128]{1,0:T(8,128)(2,1)}, bf16[512,2560]{1,0:T(8,128)(2,1)}) custom-call(bf16[128,5376]{1,0:T(8,128)(2,1)} %th_own.1, bf16[128,2560]{1,0:T(8,128)(2,1)} %sh_own.1, bf16[512,5376]{1,0:T(8,128)(2,1)} %codes.1, f32[42,512]{1,0:T(8,128)} %bitcast.3, bf16[512,2560]{1,0:T(8,128)(2,1)} %weight.1, bf16[128]{0:T(256)(128)(2,1)} %loss_in.1), custom_call_target="tpu_custom_call" | custom-call | tf_op jit(solution)/shard_map/distill/pallas_call | solution.py:517
  64.4 2.7 %hand_over.1 = (f32[1,128]{1,0:T(1,128)}, bf16[320,128]{1,0:T(8,128)(2,1)}, bf16[512,2560]{1,0:T(8,128)(2,1)}) custom-call(f32[1,128]{1,0:T(1,128)} %get-tuple-element.9.kl_in, bf16[320,128]{1,0:T(8,128)(2,1)} %get-tuple-element.10.gh_in, bf16[512,2560]{1,0:T(8,128)(2,1)} %get-tuple-element.11.gw_in), custom_call_target="tpu_custom_call" | custom-call | tf_op jit(solution)/shard_map/hand_over/pallas_call | solution.py:488
